TPU v7x, 128 devices: a whole 4x4x4 slice. The times are simulated.
128 devices in a mesh: wide: 16 (over x_lo, y, core), narrow: 8 (over z, x_hi).
Axes of the slice: x: 4 (x_hi: 2, x_lo: 2; x = x_hi * 2 + x_lo), y: 4, z: 4, core: 2. Of those that a mesh axis runs over, the one named last changes fastest.
Arguments:
- tokens: bfloat16 [4096, 2048], P('wide', 'narrow'), may hold values from -6 to 6
- norm_gain: bfloat16 [2048], replicated, may hold values from 0.25 to 1.75
- router: bfloat16 [2048, 8], replicated, may hold values from -0.125 to 0.125
- routes: int32 [4096, 2], P('wide'), may hold values from 0 to 7, all different within a row
- kv_weight: bfloat16 [4096, 2048], P('narrow', 'wide'), may hold values from -0.125 to 0.125
- query_weight: bfloat16 [16384, 2048], P('narrow', 'wide'), may hold values from -0.125 to 0.125
- out_weight: bfloat16 [16384, 2048], P('narrow', 'wide'), may hold values from -0.09375 to 0.09375
- prefix_cache: bfloat16 [12288, 4096], P('wide', 'narrow'), may hold values from -225 to 225
- suffix_lengths: int32 [4], replicated, may hold values from 1 to 3328, 4096 in all
- prefix_lengths: int32 [4], replicated, may hold values from 1 to 6144, 12288 in all
Outputs:
- mixed: bfloat16 [4096, 2048], P('wide', 'narrow')
Inputs may be any that keep to these rules, and one draw needn't show every extreme that they name: `routes`: each token names 2 different experts. `suffix_lengths`: they sum to 4096. `prefix_lengths`: they sum to 12288.
All inputs are finite; a program needn't handle non-finite values.
Results may differ from a plain program's by a relative error of at most 0.012.
The roundings to bfloat16 on the way count: a program that leaves them out, or rounds other values in their place, can miss the bound.
Values may be sent and summed in bfloat16 or wider, within the bound.
No kernel may reach another device: no remote copies, remote signals or barrier semaphores. Data moves between devices by JAX's collectives and lax.ppermute only.
A program may use at most 320 MiB of HBM per device.

v0:
```python
import math
import jax
import jax.numpy as jnp
from jax import lax
from jax.sharding import PartitionSpec as P

H = 128
E = 8
eps = 1e-06
floor_value = -1e30


def tenant_of(positions, lengths):
    bounds = jnp.cumsum(lengths)
    return jnp.sum((positions[:, None] >= bounds[None, :]).astype(jnp.int32), axis=1)


def attend(carried, queries, key_block, value_block, allowed, scaling):
    highest, totals, summed = carried
    scores = (
        jnp.einsum("hrd,nhd->hrn", queries, key_block, preferred_element_type=jnp.float32) * scaling
    )
    scores = jnp.where(allowed[None, :, :], scores, -jnp.inf)
    new_highest = jnp.maximum(highest, jnp.max(scores, axis=2))
    weights = jnp.exp(scores - new_highest[:, :, None])
    factor = jnp.exp(highest - new_highest)
    totals = totals * factor + jnp.sum(weights, axis=2)
    summed = summed * factor[:, :, None] + jnp.einsum(
        "hrn,nhd->hrd",
        weights,
        value_block.astype(jnp.float32),
        precision=lax.Precision.HIGHEST,
        preferred_element_type=jnp.float32,
    )
    return (new_highest, totals, summed)


def over_blocks(
    carried, queries, cache_rows, row_tenant, row_index, key_tenant, key_index, scaling, causal
):
    length = cache_rows.shape[0]
    block_size = math.gcd(length, 512)
    steps_count = length // block_size
    cache_blocks = cache_rows.reshape((steps_count, block_size) + cache_rows.shape[1:])
    tenant_blocks = key_tenant.reshape(steps_count, block_size)
    index_blocks = key_index.reshape(steps_count, block_size)

    def advance(current, inputs):
        rows_here, tenant_here, index_here = inputs
        allowed = row_tenant[:, None] == tenant_here[None, :]
        if causal:
            allowed = allowed & (index_here[None, :] <= row_index[:, None])
        return (
            attend(
                current, queries, rows_here[:, :, 0, :], rows_here[:, :, 1, :], allowed, scaling
            ),
            None,
        )

    carried, unused = lax.scan(advance, carried, (cache_blocks, tenant_blocks, index_blocks))
    return carried


def on_device(
    tokens,
    norm_gain,
    router,
    routes,
    kv_weight,
    query_weight,
    out_weight,
    prefix_cache,
    suffix_lengths,
    prefix_lengths,
):
    whole = lax.all_gather(tokens, "narrow", axis=1, tiled=True)
    tok_rows = whole.shape[0]
    local_heads = kv_weight.shape[0] // (2 * H)
    slot_count = routes.shape[1]
    scaling = H ** (-0.5)
    floats = whole.astype(jnp.float32)
    normed = (
        floats
        * lax.rsqrt(jnp.mean(floats * floats, axis=1, keepdims=True) + eps)
        * norm_gain.astype(jnp.float32)
    ).astype(jnp.bfloat16)
    logits = jnp.dot(normed, router, preferred_element_type=jnp.float32)
    one_hot = routes[:, :, None] == jnp.arange(E, dtype=jnp.int32)[None, None, :]
    chosen = jnp.sum(jnp.where(one_hot, logits[:, None, :], 0.0), axis=2)
    gate_values = jax.nn.softmax(chosen, axis=1)
    choose = one_hot.astype(jnp.bfloat16)
    kv_part = lax.dot_general(
        normed,
        lax.all_gather(kv_weight, "wide", axis=1, tiled=True),
        (((1,), (1,)), ((), ())),
        preferred_element_type=jnp.float32,
    )
    query_part = lax.dot_general(
        normed,
        lax.all_gather(query_weight, "wide", axis=1, tiled=True),
        (((1,), (1,)), ((), ())),
        preferred_element_type=jnp.float32,
    )
    kv_local = kv_part.astype(jnp.bfloat16).reshape(tok_rows, local_heads, 2, H)
    query_all = query_part.astype(jnp.bfloat16).reshape(tok_rows, local_heads, E, H)
    selected = jnp.einsum(
        "tje,thed->htjd", choose, query_all, preferred_element_type=jnp.float32
    ).astype(jnp.bfloat16)
    row_count = tok_rows * slot_count
    queries = selected.reshape(local_heads, row_count, H)
    first_token = lax.axis_index("wide") * tok_rows
    token_index = first_token + jnp.arange(tok_rows, dtype=jnp.int32)
    row_index = jnp.repeat(token_index, slot_count)
    row_tenant = tenant_of(row_index, suffix_lengths)
    start_carry = (
        jnp.full((local_heads, row_count), floor_value, jnp.float32),
        jnp.zeros((local_heads, row_count), jnp.float32),
        jnp.zeros((local_heads, row_count, H), jnp.float32),
    )
    shard_piece = lax.all_gather(prefix_cache, "wide", axis=0, tiled=True)
    piece_rows = shard_piece.shape[0]
    slot_index = jnp.arange(piece_rows, dtype=jnp.int32)
    slot_tenant = tenant_of(slot_index, prefix_lengths)
    cache_rows = shard_piece.reshape(piece_rows, local_heads, 2, H)
    carried = over_blocks(
        start_carry,
        queries,
        cache_rows,
        row_tenant,
        row_index,
        slot_tenant,
        slot_index,
        scaling,
        False,
    )
    shard_piece = lax.all_gather(kv_local, "wide", axis=0, tiled=True)
    piece_rows = shard_piece.shape[0]
    key_index = jnp.arange(piece_rows, dtype=jnp.int32)
    key_tenant = tenant_of(key_index, suffix_lengths)
    carried = over_blocks(
        carried, queries, shard_piece, row_tenant, row_index, key_tenant, key_index, scaling, True
    )
    highest, totals, summed = carried
    attended = (summed / totals[:, :, None]).reshape(local_heads, tok_rows, slot_count, H)
    weighted = (attended * gate_values[None, :, :, None]).astype(jnp.bfloat16)
    padded = (
        jnp.einsum("tje,htjd->thed", choose, weighted, preferred_element_type=jnp.float32)
        .astype(jnp.bfloat16)
        .reshape(tok_rows, local_heads * E * H)
    )
    partial_out = jnp.dot(
        padded,
        lax.all_gather(out_weight, "wide", axis=1, tiled=True),
        preferred_element_type=jnp.float32,
    )
    return lax.psum_scatter(partial_out, "narrow", scatter_dimension=1, tiled=True).astype(
        jnp.bfloat16
    )


def solution(mesh):
    placed = (
        P("wide", "narrow"),
        P(),
        P(),
        P("wide", None),
        P("narrow", "wide"),
        P("narrow", "wide"),
        P("narrow", "wide"),
        P("wide", "narrow"),
        P(),
        P(),
    )
    return jax.shard_map(
        on_device, mesh=mesh, in_specs=placed, out_specs=P("wide", "narrow"), check_vma=False
    )
```

profile of v0, /device:TPU:0, one launch (start us, length us, event | category | flops | bytes accessed | tf_op | source)
XLA Modules:
  0.0 498.0 jit_solution(3596680702898717761)
XLA Ops:
  10.1 47.4 %all-gather.9.cloned.1.call-done = bf16[256,2048]{1,0:T(8,128)(2,1)} async-done(((bf16[256,256]{1,0:T(8,128)(2,1)}), bf16[256,2048]{1,0:T(8,128)(2,1)}) %all-gather.9.cloned.1.call-update) | async-done | bytes 1048592 | tf_op jit(solution)/shard_map/all_gather | solution.py:76
  57.5 1.5 fusion.12
  59.0 35.4 %all-gather.13.cloned.1.call-done = bf16[512,2048]{1,0:T(8,128)(2,1)} async-done(((bf16[512,128]{1,0:T(8,128)(2,1)}), bf16[512,2048]{1,0:T(8,128)(2,1)}) %all-gather.13.cloned.1.call-update) | async-done | bytes 2097168 | tf_op jit(solution)/shard_map/all_gather | solution.py:94
  94.4 2.7 convolution_convert_fusion.2
  101.9 55.0 %all-gather.11.cloned.1.call-done = bf16[2048,2048]{1,0:T(8,128)(2,1)} async-done(((bf16[2048,128]{1,0:T(8,128)(2,1)}), bf16[2048,2048]{1,0:T(8,128)(2,1)}) %all-gather.11.cloned.1.call-update) | async-done | bytes 8388624 | tf_op jit(solution)/shard_map/all_gather | solution.py:100
  157.0 5.8 %fusion.15 = bf16[32,8,16,128]{3,1,2,0:T(8,128)(2,1)S(1)} fusion(bf16[2048,2048]{1,0:T(8,128)(2,1)} %all-gather.11.cloned.1.call-done, bf16[256,2048]{1,0:T(8,128)(2,1)S(1)} %copy-done.1, f32[2048]{0:T(1024)S(1)} %convert_element_type.48, f32[256]{0:T(256)S(1)} %add_rsqrt_fusion), kind=kOutput, calls=%fused_computation.41 | convolution fusion | flops 2150105088 | bytes 10494976 | tf_op jit(solution)/shard_map/dot_general | solution.py:98
  164.4 65.7 %all-gather.7.cloned.1.call-done = bf16[12288,512]{1,0:T(8,128)(2,1)} async-done(((bf16[768,512]{1,0:T(8,128)(2,1)}), bf16[12288,512]{1,0:T(8,128)(2,1)}) %all-gather.7.cloned.1.call-update) | async-done | bytes 12582928 | tf_op jit(solution)/shard_map/all_gather | solution.py:120
  230.1 18.2 %reshape.233 = bf16[24,512,2,2,128]{4,3,2,1,0:T(2,128)(2,1)} reshape(bf16[12288,512]{1,0:T(8,128)(2,1)} %all-gather.7.cloned.1.call-done) | data formatting | bytes 25165824 | tf_op jit(solution)/shard_map/reshape;reshape | solution.py:44
  248.3 112.6 %while.31 = (s32[]{:T(128)}, f32[2,512]{1,0:T(2,128)S(1)}, f32[2,512]{1,0:T(2,128)S(1)}, f32[2,512,128]{2,1,0:T(8,128)S(1)}, s32[512]{0:T(512)S(1)}, /*index=5*/...) while((s32[]{:T(128)}, f32[2,512]{1,0:T(2,128)S(1)}, ...), condition=%wide.region_8.9_spmd.clone, body=%wide.region_5.8_spmd.clone.sunk | while | flops 943330304 | bytes 11870357 | solution.py:60
  251.0 2.0 fusion.61
  253.0 1.5 constant_dynamic-slice_fusion.12
  255.7 2.0 fusion.61
  257.7 1.5 constant_dynamic-slice_fusion.12
  260.4 2.0 fusion.61
  262.4 1.5 constant_dynamic-slice_fusion.12
  265.1 2.0 fusion.61
  267.1 1.4 constant_dynamic-slice_fusion.12
  269.8 2.0 fusion.61
  271.8 1.4 constant_dynamic-slice_fusion.12
  274.5 2.0 fusion.61
  279.1 2.0 fusion.61
  281.1 1.5 constant_dynamic-slice_fusion.12
  283.8 2.0 fusion.61
  288.5 2.0 fusion.61
  290.5 1.5 constant_dynamic-slice_fusion.12
  293.2 2.0 fusion.61
  297.9 2.0 fusion.61
  302.6 2.0 fusion.61
  304.6 1.5 constant_dynamic-slice_fusion.12
  307.4 2.0 fusion.61
  312.0 2.0 fusion.61
  314.0 1.5 constant_dynamic-slice_fusion.12
  316.7 2.0 fusion.61
  318.7 1.5 constant_dynamic-slice_fusion.12
  321.4 2.0 fusion.61
  326.1 2.0 fusion.61
  328.1 1.5 constant_dynamic-slice_fusion.12
  330.8 2.0 fusion.61
  335.5 2.0 fusion.61
  340.2 2.0 fusion.61
  344.9 2.0 fusion.61
  349.6 2.0 fusion.61
  354.3 2.0 fusion.61
  358.9 2.0 fusion.61
  361.0 43.5 %while.30 = (s32[]{:T(128)}, f32[2,512]{1,0:T(2,128)S(1)}, f32[2,512]{1,0:T(2,128)S(1)}, f32[2,512,128]{2,1,0:T(8,128)S(1)}, s32[512]{0:T(512)S(1)}, /*index=5*/...) while((s32[]{:T(128)}, f32[2,512]{1,0:T(2,128)S(1)}, ...), condition=%wide.region_13.14_spmd.clone, body=%wide.region_10.13_spmd.clone.sunk | while | flops 943720448 | bytes 9789041 | solution.py:60
  362.6 1.5 fusion.53
  364.4 1.9 fusion.55
  368.0 1.5 fusion.53
  369.9 1.9 fusion.55
  373.5 1.5 fusion.53
  375.3 1.9 fusion.55
  378.9 1.5 fusion.53
  380.8 1.9 fusion.55
  384.4 1.5 fusion.53
  386.2 1.9 fusion.55
  389.8 1.5 fusion.53
  391.6 1.9 fusion.55
  395.2 1.5 fusion.53
  397.1 1.9 fusion.55
  400.7 1.5 fusion.53
  402.5 1.9 fusion.55
  406.1 7.1 %fusion.17 = f32[256,2048]{1,0:T(8,128)} fusion(bf16[2048,2048]{1,0:T(8,128)(2,1)} %all-gather.17.cloned.1.call-done, bf16[32,8,16,128]{3,2,1,0:T(8,128)(2,1)S(1)} %bitcast.97), kind=kOutput, calls=%fused_computation.45 | convolution fusion | flops 2147483648 | bytes 11534336 | tf_op jit(solution)/shard_map/dot_general | solution.py:151
  413.2 76.3 %reduce-scatter.2.cloned.1.call-done = f32[256,256]{1,0:T(8,128)} async-done(((f32[256,2048]{1,0:T(8,128)}), f32[256,256]{1,0:T(8,128)}) %reduce-scatter.2.cloned.1.call-update) | async-done | bytes 262160 | tf_op jit(solution)/shard_map/reduce_scatter | solution.py:156
  489.5 1.6 convert_element_type.58
  (380 shorter events, 74.3 us)
Async XLA Ops:
  6.5 93.3 %copy-start = (bf16[2048,8]{0,1:T(8,128)(2,1)S(1)}, bf16[2048,8]{0,1:T(8,128)(2,1)}, u32[]{:S(2)}) copy-start(bf16[2048,8]{0,1:T(8,128)(2,1)} %param.16) | copy-start | bytes 98308
  6.5 50.9 %all-gather.9.cloned.1.call-start = ((), (), s32[]{:S(2)}) async-start(), calls=%async_computation.2 | async-start | bytes 1179648 | tf_op jit(solution)/shard_map/all_gather | solution.py:76
  7.3 87.1 %all-gather.13.cloned.1.call-start = ((), (), s32[]{:S(2)}) async-start(), calls=%async_computation.4 | async-start | bytes 2228224 | tf_op jit(solution)/shard_map/all_gather | solution.py:94
  8.0 149.0 %all-gather.11.cloned.1.call-start = ((), (), s32[]{:S(2)}) async-start(), calls=%async_computation.3 | async-start | bytes 8912896 | tf_op jit(solution)/shard_map/all_gather | solution.py:100
  8.7 221.3 %all-gather.7.cloned.1.call-start = ((), (), s32[]{:S(2)}) async-start(), calls=%async_computation.1 | async-start | bytes 13369344 | tf_op jit(solution)/shard_map/all_gather | solution.py:120
  9.3 351.6 %all-gather.15.cloned.1.call-start = ((), (), s32[]{:S(2)}) async-start(), calls=%async_computation.5 | async-start | bytes 4456448 | tf_op jit(solution)/shard_map/all_gather | solution.py:136
  59.0 39.6 %copy-start.3 = (s32[256,2]{0,1:T(2,128)S(1)}, s32[256,2]{0,1:T(2,128)}, u32[]{:S(2)}) copy-start(s32[256,2]{0,1:T(2,128)} %param.17) | copy-start | bytes 6148
  59.0 39.8 %copy-start.4 = (s32[4]{0:T(128)S(1)}, s32[4]{0:T(128)}, u32[]{:S(2)}) copy-start(s32[4]{0:T(128)} %param.22) | copy-start | bytes 52
  97.1 2.3 copy-start.5
  97.1 2.8 copy-start.1
  97.9 308.1 %all-gather.17.cloned.1.call-start = ((), (), s32[]{:S(2)}) async-start(), calls=%async_computation.6 | async-start | bytes 8912896 | tf_op jit(solution)/shard_map/all_gather | solution.py:153
  98.5 391.0 %reduce-scatter.2.cloned.1.call-start = ((), (), s32[]{:S(2)}) async-start(), calls=%async_computation.7 | async-start | bytes 2359296 | tf_op jit(solution)/shard_map/reduce_scatter | solution.py:156
  248.3 1.8 copy-start.2
  253.0 1.8 copy-start.2
  257.7 1.8 copy-start.2
  262.4 1.8 copy-start.2
  267.1 1.8 copy-start.2
  271.8 1.8 copy-start.2
  276.4 1.8 copy-start.2
  281.1 1.8 copy-start.2
  285.8 1.8 copy-start.2
  290.5 1.8 copy-start.2
  295.2 1.8 copy-start.2
  299.9 1.8 copy-start.2
  304.6 1.9 copy-start.2
  309.3 1.8 copy-start.2
  314.0 1.8 copy-start.2
  318.7 1.8 copy-start.2
  323.4 1.8 copy-start.2
  328.1 1.8 copy-start.2
  332.8 1.8 copy-start.2
  337.5 1.8 copy-start.2
  342.2 1.8 copy-start.2
  346.9 1.8 copy-start.2
  351.6 1.8 copy-start.2
  356.2 1.8 copy-start.2
Sparse Core Ops, SparseCore 0:
  9.5 47.8 all-gather.8
  59.1 35.2 all-gather.12
  96.0 60.8 all-gather.10
  158.5 71.5 all-gather.6
  231.6 38.3 all-gather.14
  271.5 60.5 all-gather.16
  413.3 76.1 reduce-scatter.1
where the time goes:
time: 500 us; the launch traced here: 498 us
  waiting for transfers between devices  283 us (57%)
  matrix products  106 us (21%)
  local copies, waits for them, and re-layouts  68.3 us (14%)
  other arithmetic  24.2 us (5%)
  between operations  13.7 us (3%)
    reduce_scatter x1, waiting for transfers between devices, on_device(): lax.psum_scatter(partial_out, 'narrow', scatter_dimension=1, tiled=True)  76.3 us
    all_gather x1, waiting for transfers between devices, on_device(): shard_piece = lax.all_gather(prefix_cache, 'wide', axis=0, tiled=True)  65.7 us
    dot_general x32, matrix products, attend(): jnp.einsum('hrn,nhd->hrd', weights, value_block.astype(jnp.float32), prec...  62.4 us
    all_gather x1, waiting for transfers between devices, on_device(): lax.all_gather(query_weight, 'wide', axis=1, tiled=True)  55 us
    all_gather x1, waiting for transfers between devices, on_device(): whole = lax.all_gather(tokens, 'narrow', axis=1, tiled=True)  47.4 us
    dynamic_slice x80, local copies, waits for them, and re-layouts, over_blocks(): lax.scan(advance, carried, (cache_blocks, tenant_blocks, index_blocks))  37 us
    all_gather x1, waiting for transfers between devices, on_device(): lax.all_gather(kv_weight, 'wide', axis=1, tiled=True)  35.4 us
    dot_general x32, matrix products, attend(): jnp.einsum('hrd,nhd->hrn', queries, key_block, preferred_element_type=jnp...  25.4 us
  transfers between devices with their start and end apart: 7, of which 5 were waited for; matrix products, arithmetic and copies ran while one was open for 38% of the time, Pallas kernels for 0%

commit v1 on v0

--- a/solution.py
+++ b/solution.py
@@ -91,7 +91,12 @@
     choose = one_hot.astype(jnp.bfloat16)
     kv_part = lax.dot_general(
         normed,
-        lax.all_gather(kv_weight, "wide", axis=1, tiled=True),
+        jnp.concatenate(
+            jax.lax.all_to_all(
+                jnp.stack([kv_weight for _ in range(jax.lax.axis_size("wide"))]), "wide", 0, 0
+            ),
+            axis=1,
+        ),
         (((1,), (1,)), ((), ())),
         preferred_element_type=jnp.float32,
     )

time: 500 us -> 464 us (0.928)
  waiting for transfers between devices: 283 us -> 240 us
  starting transfers between devices: 0.23 us -> 5.92 us
    all_gather x1 -> x0, waiting for transfers between devices: 35.4 us -> none  [on_device(): lax.all_gather(kv_weight, 'wide', axis=1, tiled=True)]
    all_to_all x0 -> x1, starting transfers between devices: none -> 5.72 us  [on_device(): jax.lax.all_to_all(jnp.stack([kv_weight for _ in range(jax.lax.axis_size(...]
  transfers between devices with their start and end apart: 7 -> 7, of which waited for: 5 -> 4; matrix products, arithmetic and copies ran while one was open for 38% -> 41% of each run, Pallas kernels for 0% -> 0%
where the time goes in v1:
time: 464 us; the launch traced here: 462 us
  waiting for transfers between devices  240 us (52%)
  matrix products  105 us (23%)
  local copies, waits for them, and re-layouts  70.8 us (15%)
  other arithmetic  23.5 us (5%)
  between operations  13.7 us (3%)
  starting transfers between devices  5.92 us (1%)
    reduce_scatter x1, waiting for transfers between devices, on_device(): lax.psum_scatter(partial_out, 'narrow', scatter_dimension=1, tiled=True)  76.3 us
    all_gather x1, waiting for transfers between devices, on_device(): shard_piece = lax.all_gather(prefix_cache, 'wide', axis=0, tiled=True)  65.8 us
    dot_general x32, matrix products, attend(): jnp.einsum('hrn,nhd->hrd', weights, value_block.astype(jnp.float32), prec...  62.4 us
    all_gather x1, waiting for transfers between devices, on_device(): lax.all_gather(query_weight, 'wide', axis=1, tiled=True)  52.7 us
    all_gather x1, waiting for transfers between devices, on_device(): whole = lax.all_gather(tokens, 'narrow', axis=1, tiled=True)  42.7 us
    dynamic_slice x80, local copies, waits for them, and re-layouts, over_blocks(): lax.scan(advance, carried, (cache_blocks, tenant_blocks, index_blocks))  37 us
    dot_general x32, matrix products, attend(): jnp.einsum('hrd,nhd->hrn', queries, key_block, preferred_element_type=jnp...  25.4 us
    another operation x1, local copies, waits for them, and re-layouts, over_blocks(): cache_rows.reshape((steps_count, block_size) + cache_rows.shape[1:])  18.1 us
  transfers between devices with their start and end apart: 7, of which 4 were waited for; matrix products, arithmetic and copies ran while one was open for 41% of the time, Pallas kernels for 0%

profile of v1, /device:TPU:0, one launch (start us, length us, event | category | flops | bytes accessed | tf_op | source)
XLA Modules:
  0.0 461.9 jit_solution(13415337850883714901)
XLA Ops:
  9.8 1.5 stack.2
  11.3 5.7 %all-to-all-start = ((bf16[16,512,128]{1,2,0:T(8,128)(2,1)}), bf16[16,512,128]{1,2,0:T(8,128)(2,1)S(1)}, u32[]{:S(2)}, u32[]{:S(2)}) async-start(bf16[16,512,128]{1,2,0:T(8,128)(2,1)} %stack.2), calls=%async_computation | async-start | bytes 4194304 | tf_op jit(solution)/shard_map/all_to_all | solution.py:95
  17.1 42.7 %all-gather.8.cloned.1.call-done = bf16[256,2048]{1,0:T(8,128)(2,1)} async-done(((bf16[256,256]{1,0:T(8,128)(2,1)}), bf16[256,2048]{1,0:T(8,128)(2,1)}) %all-gather.8.cloned.1.call-update) | async-done | bytes 1048592 | tf_op jit(solution)/shard_map/all_gather | solution.py:76
  59.8 1.5 fusion.12
  61.3 2.0 convolution_convert_fusion.2
  68.2 52.7 %all-gather.10.cloned.1.call-done = bf16[2048,2048]{1,0:T(8,128)(2,1)} async-done(((bf16[2048,128]{1,0:T(8,128)(2,1)}), bf16[2048,2048]{1,0:T(8,128)(2,1)}) %all-gather.10.cloned.1.call-update) | async-done | bytes 8388624 | tf_op jit(solution)/shard_map/all_gather | solution.py:105
  120.8 5.8 %fusion.15 = bf16[32,8,16,128]{3,1,2,0:T(8,128)(2,1)S(1)} fusion(bf16[2048,2048]{1,0:T(8,128)(2,1)} %all-gather.10.cloned.1.call-done, bf16[256,2048]{1,0:T(8,128)(2,1)S(1)} %copy-done.2, f32[2048]{0:T(1024)S(1)} %convert_element_type.48, f32[256]{0:T(256)S(1)} %add_rsqrt_fusion), kind=kOutput, calls=%fused_computation.41 | convolution fusion | flops 2150105088 | bytes 10494976 | tf_op jit(solution)/shard_map/dot_general | solution.py:103
  128.3 65.8 %all-gather.6.cloned.1.call-done = bf16[12288,512]{1,0:T(8,128)(2,1)} async-done(((bf16[768,512]{1,0:T(8,128)(2,1)}), bf16[12288,512]{1,0:T(8,128)(2,1)}) %all-gather.6.cloned.1.call-update) | async-done | bytes 12582928 | tf_op jit(solution)/shard_map/all_gather | solution.py:125
  194.1 18.1 %reshape.243 = bf16[24,512,2,2,128]{4,3,2,1,0:T(2,128)(2,1)} reshape(bf16[12288,512]{1,0:T(8,128)(2,1)} %all-gather.6.cloned.1.call-done) | data formatting | bytes 25165824 | tf_op jit(solution)/shard_map/reshape;reshape | solution.py:44
  212.2 112.6 %while.31 = (s32[]{:T(128)}, f32[2,512]{1,0:T(2,128)S(1)}, f32[2,512]{1,0:T(2,128)S(1)}, f32[2,512,128]{2,1,0:T(8,128)S(1)}, s32[512]{0:T(512)S(1)}, /*index=5*/...) while((s32[]{:T(128)}, f32[2,512]{1,0:T(2,128)S(1)}, ...), condition=%wide.region_8.9_spmd.clone, body=%wide.region_5.8_spmd.clone.sunk | while | flops 943330304 | bytes 11870357 | solution.py:60
  214.9 2.0 fusion.61
  216.9 1.5 constant_dynamic-slice_fusion.12
  219.6 2.0 fusion.61
  221.6 1.5 constant_dynamic-slice_fusion.12
  224.3 2.0 fusion.61
  226.3 1.5 constant_dynamic-slice_fusion.12
  229.0 2.0 fusion.61
  231.0 1.5 constant_dynamic-slice_fusion.12
  233.7 2.0 fusion.61
  238.4 2.0 fusion.61
  243.1 2.0 fusion.61
  245.1 1.5 constant_dynamic-slice_fusion.12
  247.8 2.0 fusion.61
  252.5 2.0 fusion.61
  254.5 1.5 constant_dynamic-slice_fusion.12
  257.2 2.0 fusion.61
  261.9 2.0 fusion.61
  266.6 2.0 fusion.61
  268.5 1.5 constant_dynamic-slice_fusion.12
  271.3 2.0 fusion.61
  276.0 2.0 fusion.61
  278.0 1.5 constant_dynamic-slice_fusion.12
  280.7 2.0 fusion.61
  282.7 1.5 constant_dynamic-slice_fusion.12
  285.4 2.0 fusion.61
  290.1 2.0 fusion.61
  292.1 1.5 constant_dynamic-slice_fusion.12
  294.8 2.0 fusion.61
  299.5 2.0 fusion.61
  304.2 2.0 fusion.61
  308.8 2.0 fusion.61
  313.5 2.0 fusion.61
  318.2 2.0 fusion.61
  322.9 2.0 fusion.61
  324.9 43.5 %while.30 = (s32[]{:T(128)}, f32[2,512]{1,0:T(2,128)S(1)}, f32[2,512]{1,0:T(2,128)S(1)}, f32[2,512,128]{2,1,0:T(8,128)S(1)}, s32[512]{0:T(512)S(1)}, /*index=5*/...) while((s32[]{:T(128)}, f32[2,512]{1,0:T(2,128)S(1)}, ...), condition=%wide.region_13.14_spmd.clone, body=%wide.region_10.13_spmd.clone.sunk | while | flops 943720448 | bytes 9789041 | solution.py:60
  326.6 1.5 fusion.53
  328.4 1.9 fusion.55
  332.0 1.5 fusion.53
  333.8 1.9 fusion.55
  337.4 1.5 fusion.53
  339.3 1.9 fusion.55
  342.9 1.5 fusion.53
  344.7 1.9 fusion.55
  348.3 1.5 fusion.53
  350.2 1.9 fusion.55
  353.8 1.5 fusion.53
  355.6 1.9 fusion.55
  359.2 1.5 fusion.53
  361.0 1.9 fusion.55
  364.6 1.5 fusion.53
  366.5 1.9 fusion.55
  370.0 7.1 %fusion.17 = f32[256,2048]{1,0:T(8,128)} fusion(bf16[2048,2048]{1,0:T(8,128)(2,1)} %all-gather.14.cloned.1.call-done, bf16[32,8,16,128]{3,2,1,0:T(8,128)(2,1)S(1)} %bitcast.101), kind=kOutput, calls=%fused_computation.45 | convolution fusion | flops 2147483648 | bytes 11534336 | tf_op jit(solution)/shard_map/dot_general | solution.py:156
  377.1 76.3 %reduce-scatter.2.cloned.1.call-done = f32[256,256]{1,0:T(8,128)} async-done(((f32[256,2048]{1,0:T(8,128)}), f32[256,256]{1,0:T(8,128)}) %reduce-scatter.2.cloned.1.call-update) | async-done | bytes 262160 | tf_op jit(solution)/shard_map/reduce_scatter | solution.py:161
  453.4 1.6 convert_element_type.58
  (385 shorter events, 75.5 us)
Async XLA Ops:
  6.5 59.6 %copy-start = (bf16[2048,8]{0,1:T(8,128)(2,1)S(1)}, bf16[2048,8]{0,1:T(8,128)(2,1)}, u32[]{:S(2)}) copy-start(bf16[2048,8]{0,1:T(8,128)(2,1)} %param.16) | copy-start | bytes 98308
  6.5 53.2 %all-gather.8.cloned.1.call-start = ((), (), s32[]{:S(2)}) async-start(), calls=%async_computation.3 | async-start | bytes 1179648 | tf_op jit(solution)/shard_map/all_gather | solution.py:76
  7.3 113.6 %all-gather.10.cloned.1.call-start = ((), (), s32[]{:S(2)}) async-start(), calls=%async_computation.4 | async-start | bytes 8912896 | tf_op jit(solution)/shard_map/all_gather | solution.py:105
  8.0 186.1 %all-gather.6.cloned.1.call-start = ((), (), s32[]{:S(2)}) async-start(), calls=%async_computation.2 | async-start | bytes 13369344 | tf_op jit(solution)/shard_map/all_gather | solution.py:125
  11.3 5.8 %copy-start.4 = (bf16[2048]{0:T(1024)(128)(2,1)S(1)}, bf16[2048]{0:T(1024)(128)(2,1)}, u32[]{:S(2)}) copy-start(bf16[2048]{0:T(1024)(128)(2,1)} %param.15) | copy-start | bytes 12292
  11.3 50.0 %all-to-all-start = ((bf16[16,512,128]{1,2,0:T(8,128)(2,1)}), bf16[16,512,128]{1,2,0:T(8,128)(2,1)S(1)}, u32[]{:S(2)}, u32[]{:S(2)}) async-start(bf16[16,512,128]{1,2,0:T(8,128)(2,1)} %stack.2), calls=%async_computation | async-start | bytes 4194304 | tf_op jit(solution)/shard_map/all_to_all | solution.py:95
  17.0 307.9 %all-gather.12.cloned.1.call-start = ((), (), s32[]{:S(2)}) async-start(), calls=%async_computation.5 | async-start | bytes 4456448 | tf_op jit(solution)/shard_map/all_gather | solution.py:141
  61.3 3.6 copy-start.5
  61.3 3.7 copy-start.6
  63.3 2.3 copy-start.7
  63.3 2.8 copy-start.2
  64.2 305.8 %all-gather.14.cloned.1.call-start = ((), (), s32[]{:S(2)}) async-start(), calls=%async_computation.6 | async-start | bytes 8912896 | tf_op jit(solution)/shard_map/all_gather | solution.py:158
  64.8 388.6 %reduce-scatter.2.cloned.1.call-start = ((), (), s32[]{:S(2)}) async-start(), calls=%async_computation.7 | async-start | bytes 2359296 | tf_op jit(solution)/shard_map/reduce_scatter | solution.py:161
  212.2 1.8 copy-start.3
  216.9 1.8 copy-start.3
  221.6 1.8 copy-start.3
  226.3 1.8 copy-start.3
  231.0 1.8 copy-start.3
  235.7 1.8 copy-start.3
  240.4 1.8 copy-start.3
  245.1 1.8 copy-start.3
  249.8 1.8 copy-start.3
  254.5 1.8 copy-start.3
  259.2 1.8 copy-start.3
  263.9 1.8 copy-start.3
  268.5 1.9 copy-start.3
  273.3 1.8 copy-start.3
  278.0 1.8 copy-start.3
  282.7 1.8 copy-start.3
  287.4 1.8 copy-start.3
  292.1 1.8 copy-start.3
  296.8 1.8 copy-start.3
  301.5 1.8 copy-start.3
  306.1 1.8 copy-start.3
  310.8 1.8 copy-start.3
  315.5 1.8 copy-start.3
  320.2 1.8 copy-start.3
  370.0 85.0 %copy-start.1 = (bf16[2048,8]{0,1:T(8,128)(2,1)S(1)}, bf16[2048,8]{0,1:T(8,128)(2,1)}, u32[]{:S(2)}) copy-start(bf16[2048,8]{0,1:T(8,128)(2,1)} %param.16) | copy-start | bytes 98308
Sparse Core Ops, SparseCore 0:
  9.5 50.1 all-gather.7
  61.4 59.3 all-gather.9
  122.5 71.5 all-gather.5
  195.6 38.3 all-gather.11
  235.5 60.5 all-gather.13
  377.3 76.1 reduce-scatter.1
